TPU v7x, 32 devices: a whole 2x2x4 slice. The times are simulated.
32 devices in a mesh: dp: 8 (over z, x), mp: 4 (over y, core).
Axes of the slice: x: 2, y: 2, z: 4, core: 2. Of those that a mesh axis runs over, the one named last changes fastest.
Arguments:
- activations: bfloat16 [4096, 3072], P('dp', 'mp'), may hold values from -6 to 6
- out_grads: bfloat16 [4096, 6144], P('dp', 'mp'), may hold values from -0.25 to 0.25
- error: bfloat16 [8, 3072, 6144], P('dp', 'mp'), may hold values from -8 to 8
- sketch: bfloat16 [6144, 64], replicated, may hold values from -0.078125 to 0.078125
- momentum: float32 [3072, 6144], P('mp', 'dp'), may hold values from -6 to 6
Outputs:
- error_new: bfloat16 [8, 3072, 6144], P('dp', 'mp')
- momentum_new: float32 [3072, 6144], P('mp', 'dp')
- next_sketch: bfloat16 [6144, 64], replicated
All inputs are finite; a program needn't handle non-finite values.
Results may differ from a plain program's by a relative error of at most 0.0057.
Values may be sent and summed in bfloat16 or wider, within the bound.
A program may use at most 64 MiB of HBM per device.

v0:
```python
import jax
import jax.numpy as jnp
from jax import lax
from jax.sharding import PartitionSpec as P

beta_decay = 0.9


def update_momentum(momentum, basis_rows, sketch_block):
    product = lax.dot_general(
        basis_rows, sketch_block, (((1,), (1,)), ((), ())), preferred_element_type=jnp.float32
    )
    return beta_decay * momentum + product


def local(activations, out_grads, error, sketch, momentum):
    own_error = error[0]
    product = lax.dot_general(
        activations,
        lax.all_gather(out_grads, "mp", axis=1, tiled=True),
        (((0,), (0,)), ((), ())),
        preferred_element_type=jnp.float32,
    )
    accumulated = (product + own_error.astype(jnp.float32)).astype(jnp.bfloat16)
    local_left = jnp.dot(accumulated, sketch, preferred_element_type=jnp.float32)
    left_sketch = lax.psum(local_left, "dp")
    gram_local = jnp.dot(
        left_sketch.T,
        left_sketch,
        precision=lax.Precision.HIGHEST,
        preferred_element_type=jnp.float32,
    )
    gram_matrix = lax.psum(gram_local, "mp")
    factor = jnp.linalg.cholesky(gram_matrix)
    basis_rows = jax.scipy.linalg.solve_triangular(factor, left_sketch.T, lower=True).T.astype(
        jnp.bfloat16
    )
    block_width = momentum.shape[1]
    local_right = lax.dot_general(
        accumulated, basis_rows, (((0,), (0,)), ((), ())), preferred_element_type=jnp.float32
    )
    right_sketch = lax.psum(local_right, ("dp", "mp"))
    next_sketch = right_sketch.astype(jnp.bfloat16)
    sketch_part = lax.dynamic_slice_in_dim(
        next_sketch, lax.axis_index("dp") * block_width, block_width, 0
    )
    momentum_new = update_momentum(momentum, basis_rows, sketch_part)
    decoded = lax.dot_general(
        basis_rows, next_sketch, (((1,), (1,)), ((), ())), preferred_element_type=jnp.float32
    )
    error_new = (accumulated.astype(jnp.float32) - decoded / lax.axis_size("dp")).astype(
        jnp.bfloat16
    )
    return (error_new[None], momentum_new, next_sketch)


def solution(mesh):
    in_specs = (P("dp", "mp"), P("dp", "mp"), P("dp", "mp", None), P(), P("mp", "dp"))
    out_specs = (P("dp", "mp", None), P("mp", "dp"), P())
    return jax.shard_map(local, mesh=mesh, in_specs=in_specs, out_specs=out_specs, check_vma=False)
```

profile of v0, /device:TPU:0, one launch (start us, length us, event | category | flops | bytes accessed | tf_op | source)
XLA Modules:
  0.0 249.4 jit_solution(14047941913646381180)
XLA Ops:
  7.2 0.0 copy-start
  7.2 0.0 all-gather.2.cloned.1.call-start
  7.2 0.7 all-gather.2.cloned.1.call-update
  7.9 0.0 copy-start.4
  7.9 0.0 all-reduce.3.cloned.1.call-start
  8.0 50.7 %all-gather.2.cloned.1.call-done = bf16[512,6144]{1,0:T(8,128)(2,1)} async-done(((bf16[512,1536]{1,0:T(8,128)(2,1)}), bf16[512,6144]{1,0:T(8,128)(2,1)}) %all-gather.2.cloned.1.call-update) | async-done | bytes 6291472 | tf_op jit(solution)/shard_map/all_gather | solution.py:20
  58.7 0.0 copy-done
  58.7 9.6 %fusion = bf16[768,6144]{1,0:T(8,128)(2,1)S(1)} fusion(bf16[1,768,6144]{2,1,0:T(8,128)(2,1)} %param.7, bf16[512,768]{1,0:T(8,128)(2,1)S(1)} %copy-done, bf16[512,6144]{1,0:T(8,128)(2,1)} %all-gather.2.cloned.1.call-done), kind=kOutput, calls=%fused_computation.1 | convolution fusion | flops 4845993984 | bytes 25952256 | tf_op jit(solution)/shard_map/dot_general | solution.py:18
  68.3 0.0 copy-start.1
  68.3 3.7 %copy-done.1 = bf16[768,6144]{1,0:T(8,128)(2,1)} copy-done((bf16[768,6144]{1,0:T(8,128)(2,1)}, bf16[768,6144]{1,0:T(8,128)(2,1)S(1)}, u32[]{:S(2)}) %copy-start.1) | copy-done | bytes 9437208
  72.1 0.0 copy-done.4
  72.1 3.7 %fusion.7 = f32[768,64]{0,1:T(8,128)} fusion(bf16[768,6144]{1,0:T(8,128)(2,1)S(1)} %fusion, bf16[6144,64]{0,1:T(8,128)(2,1)S(1)} %copy-done.4), kind=kOutput, calls=%fused_computation.17 | convolution fusion | flops 603979776 | bytes 10420224 | tf_op jit(solution)/shard_map/dot_general | solution.py:25
  75.7 0.0 all-reduce.3.cloned.1.call-update
  75.8 70.8 %all-reduce.3.cloned.1.call-done = f32[768,64]{0,1:T(8,128)} async-done(((f32[768,64]{0,1:T(8,128)}), f32[768,64]{0,1:T(8,128)}) %all-reduce.3.cloned.1.call-update) | async-done | bytes 196624 | tf_op jit(solution)/shard_map/psum | solution.py:26
  146.6 1.3 fusion.8
  147.9 10.3 %psum.22 = f32[64,64]{0,1:T(8,128)S(1)} all-reduce(f32[64,64]{0,1:T(8,128)S(1)} %fusion.8), channel_id=1, replica_groups=mesh['dp'=8,'mp'=4] {'mp'}, use_global_device_ids=true, to_apply=%region_1.0 | all-reduce | flops 4096 | bytes 32768 | tf_op jit(solution)/shard_map/psum | solution.py:33
  158.2 0.1 copy.9
  158.3 5.8 %cholesky.16 = f32[64,64]{1,0:T(8,128)S(1)} custom-call(f32[64,64]{1,0:T(8,128)S(1)} %fusion.5), custom_call_target="Cholesky" | custom-call | tf_op jit(solution)/shard_map/jit(cholesky)/cholesky | solution.py:34
  164.2 0.6 compare_reduce_fusion
  164.8 0.7 fusion.3
  165.5 4.9 %custom-call.7 = f32[1,64,64]{1,2,0:T(8,128)S(1)} custom-call(f32[1,64,64]{2,1,0:T(8,128)S(1)} %fusion.3), custom_call_target="InvertDiagBlocksLowerTriangular" | custom-call | tf_op jit(solution)/shard_map/jit(_solve_triangular)/triangular_solve | solution.py:35
  170.4 1.3 convolution_convert_fusion
  171.7 5.4 %fusion.9 = f32[6144,64]{0,1:T(8,128)S(1)} fusion(bf16[768,64]{0,1:T(8,128)(2,1)S(1)} %convolution_convert_fusion, bf16[768,6144]{1,0:T(8,128)(2,1)} %copy-done.1), kind=kOutput, calls=%fused_computation.19 | convolution fusion | flops 603979776 | bytes 11108352 | tf_op jit(solution)/shard_map/dot_general | solution.py:39
  177.1 55.7 %all-reduce.4 = bf16[6144,64]{0,1:T(8,128)(2,1)S(1)} all-reduce(f32[6144,64]{0,1:T(8,128)S(1)} %fusion.9), channel_id=1, replica_groups=mesh['dp'=8,'mp'=4] {'dp','mp'}, use_global_device_ids=true, to_apply=%region_4.5 | all-reduce | flops 393216 | bytes 2359296 | tf_op jit(solution)/shard_map/psum | solution.py:42
  232.8 0.0 copy-start.2
  232.8 0.0 copy-start.3
  232.8 7.8 %fusion.1 = bf16[1,768,6144]{2,1,0:T(8,128)(2,1)} fusion(bf16[768,64]{0,1:T(8,128)(2,1)S(1)} %convolution_convert_fusion, bf16[6144,64]{0,1:T(8,128)(2,1)S(1)} %all-reduce.4, bf16[768,6144]{1,0:T(8,128)(2,1)} %copy-done.1), kind=kOutput, calls=%fused_computation.3 | convolution fusion | flops 622854144 | bytes 19759104 | tf_op jit(solution)/shard_map/dot_general | solution.py:48
  240.7 0.0 copy-done.2
  240.7 0.0 copy-done.3
  240.7 1.9 multiply_add_fusion
  (2 shorter events, 0.0 us)
Async XLA Ops:
  7.2 51.5 %copy-start = (bf16[512,768]{1,0:T(8,128)(2,1)S(1)}, bf16[512,768]{1,0:T(8,128)(2,1)}, u32[]{:S(2)}) copy-start(bf16[512,768]{1,0:T(8,128)(2,1)} %param.5) | copy-start | bytes 2359300
  7.2 51.5 %all-gather.2.cloned.1.call-start = ((), (), s32[]{:S(2)}) async-start(), calls=%async_computation | async-start | bytes 7864320 | tf_op jit(solution)/shard_map/all_gather | solution.py:20
  7.9 64.2 %copy-start.4 = (bf16[6144,64]{0,1:T(8,128)(2,1)S(1)}, bf16[6144,64]{0,1:T(8,128)(2,1)}, u32[]{:S(2)}) copy-start(bf16[6144,64]{0,1:T(8,128)(2,1)} %param.8) | copy-start | bytes 2359300
  7.9 138.7 %all-reduce.3.cloned.1.call-start = ((), (), s32[]{:S(2)}) async-start(), calls=%async_computation.1 | async-start | bytes 393216 | tf_op jit(solution)/shard_map/psum | solution.py:26
  68.3 3.7 %copy-start.1 = (bf16[768,6144]{1,0:T(8,128)(2,1)}, bf16[768,6144]{1,0:T(8,128)(2,1)S(1)}, u32[]{:S(2)}) copy-start(bf16[768,6144]{1,0:T(8,128)(2,1)S(1)} %fusion) | copy-start | bytes 28311556
  232.8 7.8 %copy-start.2 = (bf16[6144,64]{0,1:T(8,128)(2,1)}, bf16[6144,64]{0,1:T(8,128)(2,1)S(1)}, u32[]{:S(2)}) copy-start(bf16[6144,64]{0,1:T(8,128)(2,1)S(1)} %all-reduce.4) | copy-start | bytes 2359300
  232.8 7.8 %copy-start.3 = (f32[768,768]{1,0:T(8,128)S(1)}, f32[768,768]{1,0:T(8,128)}, u32[]{:S(2)}) copy-start(f32[768,768]{1,0:T(8,128)} %param.9) | copy-start | bytes 7077892
Sparse Core Ops, SparseCore 0:
  9.5 49.0 all-gather.1
  75.9 70.6 all-reduce.2
where the time goes:
time: 250 us; the launch traced here: 249 us
  waiting for transfers between devices  122 us (49%)
  blocking collectives  66 us (26%)
  matrix products  31.1 us (12%)
  between operations  14.2 us (6%)
  other arithmetic  12.1 us (5%)
  local copies, waits for them, and re-layouts  3.84 us (2%)
    psum x1, waiting for transfers between devices, local(): left_sketch = lax.psum(local_left, 'dp')  70.8 us
    psum x1, blocking collectives, local(): right_sketch = lax.psum(local_right, ('dp', 'mp'))  55.7 us
    all_gather x1, waiting for transfers between devices, local(): lax.all_gather(out_grads, 'mp', axis=1, tiled=True)  50.7 us
    psum x1, blocking collectives, local(): gram_matrix = lax.psum(gram_local, 'mp')  10.3 us
    dot_general x1, matrix products, local(): lax.dot_general(activations, lax.all_gather(out_grads, 'mp', axis=1, tile...  9.64 us
    dot_general x1, matrix products, local(): lax.dot_general(basis_rows, next_sketch, (((1,), (1,)), ((), ())), prefer...  7.81 us
    another operation x3, other arithmetic, local(): factor = jnp.linalg.cholesky(gram_matrix)  6.52 us
    another operation x2, other arithmetic, local(): jax.scipy.linalg.solve_triangular(factor, left_sketch.T, lower=True)  5.55 us
  transfers between devices with their start and end apart: 2, of which 2 were waited for; matrix products, arithmetic and copies ran while one was open for 0% of the time, Pallas kernels for 0%

commit v1 on v0

--- a/solution.py
+++ b/solution.py
@@ -23,7 +23,7 @@
     )
     accumulated = (product + own_error.astype(jnp.float32)).astype(jnp.bfloat16)
     local_left = jnp.dot(accumulated, sketch, preferred_element_type=jnp.float32)
-    left_sketch = lax.psum(local_left, "dp")
+    left_sketch = jnp.sum(lax.all_gather(local_left, "dp"), axis=0)
     gram_local = jnp.dot(
         left_sketch.T,
         left_sketch,

time: 250 us -> 224 us (0.90)
  waiting for transfers between devices: 122 us -> 95.7 us
    psum x1 -> x0, waiting for transfers between devices: 70.8 us -> none  [local(): left_sketch = lax.psum(local_left, 'dp')]
    all_gather x0 -> x1, waiting for transfers between devices: none -> 44.3 us  [local(): left_sketch = jnp.sum(lax.all_gather(local_left, 'dp'), axis=0)]
    unnamed x10 -> x11, local copies, waits for them, and re-layouts: 3.76 us -> 5.64 us
where the time goes in v1:
time: 224 us
  waiting for transfers between devices  95.7 us (43%)
  blocking collectives  66.5 us (30%)
  matrix products  29.1 us (13%)
  between operations  14.2 us (6%)
  other arithmetic  12.5 us (6%)
  local copies, waits for them, and re-layouts  5.72 us (3%)
    psum x1, blocking collectives, local(): right_sketch = lax.psum(local_right, ('dp', 'mp'))  56.2 us
    all_gather x1, waiting for transfers between devices, local(): lax.all_gather(out_grads, 'mp', axis=1, tiled=True)  50.7 us
    all_gather x1, waiting for transfers between devices, local(): left_sketch = jnp.sum(lax.all_gather(local_left, 'dp'), axis=0)  44.3 us
    psum x1, blocking collectives, local(): gram_matrix = lax.psum(gram_local, 'mp')  10.3 us
    dot_general x1, matrix products, local(): lax.dot_general(activations, lax.all_gather(out_grads, 'mp', axis=1, tile...  9.64 us
    dot_general x1, matrix products, local(): lax.dot_general(basis_rows, next_sketch, (((1,), (1,)), ((), ())), prefer...  7.82 us
    another operation x3, other arithmetic, local(): factor = jnp.linalg.cholesky(gram_matrix)  6.52 us
    unnamed x11, local copies, waits for them, and re-layouts  5.64 us
  transfers between devices with their start and end apart: 2, of which 2 were waited for; matrix products, arithmetic and copies ran while one was open for 0% of the time, Pallas kernels for 0%

profile of v1, /device:TPU:0, one launch (start us, length us, event | category | flops | bytes accessed | tf_op | source)
XLA Modules:
  0.0 223.8 jit_solution(8009464143487280420)
XLA Ops:
  7.2 0.0 copy-start
  7.2 0.0 all-gather.4.cloned.1.call-start
  7.2 0.7 all-gather.4.cloned.1.call-update
  7.9 0.0 copy-start.4
  7.9 0.0 all-gather.6.cloned.1.call-start
  8.0 50.7 %all-gather.4.cloned.1.call-done = bf16[512,6144]{1,0:T(8,128)(2,1)} async-done(((bf16[512,1536]{1,0:T(8,128)(2,1)}), bf16[512,6144]{1,0:T(8,128)(2,1)}) %all-gather.4.cloned.1.call-update) | async-done | bytes 6291472 | tf_op jit(solution)/shard_map/all_gather | solution.py:20
  58.7 0.0 copy-done
  58.7 9.6 %fusion = bf16[768,6144]{1,0:T(8,128)(2,1)S(1)} fusion(bf16[1,768,6144]{2,1,0:T(8,128)(2,1)} %param.7, bf16[512,768]{1,0:T(8,128)(2,1)S(1)} %copy-done, bf16[512,6144]{1,0:T(8,128)(2,1)} %all-gather.4.cloned.1.call-done), kind=kOutput, calls=%fused_computation.1 | convolution fusion | flops 4845993984 | bytes 25952256 | tf_op jit(solution)/shard_map/dot_general | solution.py:18
  68.3 0.0 copy-start.1
  68.3 3.7 %copy-done.1 = bf16[768,6144]{1,0:T(8,128)(2,1)} copy-done((bf16[768,6144]{1,0:T(8,128)(2,1)}, bf16[768,6144]{1,0:T(8,128)(2,1)S(1)}, u32[]{:S(2)}) %copy-start.1) | copy-done | bytes 9437208
  72.1 0.0 copy-done.4
  72.1 3.7 %fusion.7 = f32[768,64]{0,1:T(8,128)} fusion(bf16[768,6144]{1,0:T(8,128)(2,1)S(1)} %fusion, bf16[6144,64]{0,1:T(8,128)(2,1)S(1)} %copy-done.4), kind=kOutput, calls=%fused_computation.18 | convolution fusion | flops 603979776 | bytes 10420224 | tf_op jit(solution)/shard_map/dot_general | solution.py:25
  75.7 0.0 all-gather.6.cloned.1.call-update
  75.7 44.3 %all-gather.6.cloned.1.call-done = f32[6144,64]{0,1:T(8,128)} async-done(((f32[768,64]{0,1:T(8,128)}), f32[6144,64]{0,1:T(8,128)}) %all-gather.6.cloned.1.call-update) | async-done | bytes 1572880 | tf_op jit(solution)/shard_map/all_gather | solution.py:26
  120.1 1.9 copy.13
  122.0 0.4 bitcast_reduce_fusion
  122.4 0.3 fusion.8
  122.7 10.3 %psum.14 = f32[64,64]{0,1:T(8,128)S(1)} all-reduce(f32[64,64]{0,1:T(8,128)S(1)} %fusion.8), channel_id=1, replica_groups=mesh['dp'=8,'mp'=4] {'mp'}, use_global_device_ids=true, to_apply=%region_1.0 | all-reduce | flops 4096 | bytes 32768 | tf_op jit(solution)/shard_map/psum | solution.py:33
  133.0 0.1 copy.11
  133.0 5.8 %cholesky.16 = f32[64,64]{1,0:T(8,128)S(1)} custom-call(f32[64,64]{1,0:T(8,128)S(1)} %fusion.5), custom_call_target="Cholesky" | custom-call | tf_op jit(solution)/shard_map/jit(cholesky)/cholesky | solution.py:34
  138.9 0.6 compare_reduce_fusion
  139.6 0.7 fusion.3
  140.2 4.9 %custom-call.7 = f32[1,64,64]{1,2,0:T(8,128)S(1)} custom-call(f32[1,64,64]{2,1,0:T(8,128)S(1)} %fusion.3), custom_call_target="InvertDiagBlocksLowerTriangular" | custom-call | tf_op jit(solution)/shard_map/jit(_solve_triangular)/triangular_solve | solution.py:35
  145.1 0.4 convolution_convert_fusion
  145.5 5.4 %fusion.9 = f32[6144,64]{0,1:T(8,128)S(1)} fusion(bf16[768,64]{0,1:T(8,128)(2,1)S(1)} %convolution_convert_fusion, bf16[768,6144]{1,0:T(8,128)(2,1)} %copy-done.1), kind=kOutput, calls=%fused_computation.20 | convolution fusion | flops 603979776 | bytes 11108352 | tf_op jit(solution)/shard_map/dot_general | solution.py:39
  151.0 56.2 %all-reduce.1 = bf16[6144,64]{0,1:T(8,128)(2,1)S(1)} all-reduce(f32[6144,64]{0,1:T(8,128)S(1)} %fusion.9), channel_id=1, replica_groups=mesh['dp'=8,'mp'=4] {'dp','mp'}, use_global_device_ids=true, to_apply=%region_4.5 | all-reduce | flops 393216 | bytes 2359296 | tf_op jit(solution)/shard_map/psum | solution.py:42
  207.2 0.0 copy-start.2
  207.2 0.0 copy-start.3
  207.2 7.8 %fusion.1 = bf16[1,768,6144]{2,1,0:T(8,128)(2,1)} fusion(bf16[768,64]{0,1:T(8,128)(2,1)S(1)} %convolution_convert_fusion, bf16[6144,64]{0,1:T(8,128)(2,1)S(1)} %all-reduce.1, bf16[768,6144]{1,0:T(8,128)(2,1)} %copy-done.1), kind=kOutput, calls=%fused_computation.3 | convolution fusion | flops 622854144 | bytes 19759104 | tf_op jit(solution)/shard_map/dot_general | solution.py:48
  215.0 0.0 copy-done.2
  215.0 0.0 copy-done.3
  215.0 1.9 multiply_add_fusion
  (2 shorter events, 0.0 us)
Async XLA Ops:
  7.2 51.5 %copy-start = (bf16[512,768]{1,0:T(8,128)(2,1)S(1)}, bf16[512,768]{1,0:T(8,128)(2,1)}, u32[]{:S(2)}) copy-start(bf16[512,768]{1,0:T(8,128)(2,1)} %param.5) | copy-start | bytes 2359300
  7.2 51.5 %all-gather.4.cloned.1.call-start = ((), (), s32[]{:S(2)}) async-start(), calls=%async_computation | async-start | bytes 7864320 | tf_op jit(solution)/shard_map/all_gather | solution.py:20
  7.9 64.2 %copy-start.4 = (bf16[6144,64]{0,1:T(8,128)(2,1)S(1)}, bf16[6144,64]{0,1:T(8,128)(2,1)}, u32[]{:S(2)}) copy-start(bf16[6144,64]{0,1:T(8,128)(2,1)} %param.8) | copy-start | bytes 2359300
  7.9 112.2 %all-gather.6.cloned.1.call-start = ((), (), s32[]{:S(2)}) async-start(), calls=%async_computation.1 | async-start | bytes 1769472 | tf_op jit(solution)/shard_map/all_gather | solution.py:26
  68.3 3.7 %copy-start.1 = (bf16[768,6144]{1,0:T(8,128)(2,1)}, bf16[768,6144]{1,0:T(8,128)(2,1)S(1)}, u32[]{:S(2)}) copy-start(bf16[768,6144]{1,0:T(8,128)(2,1)S(1)} %fusion) | copy-start | bytes 28311556
  207.2 7.8 %copy-start.2 = (bf16[6144,64]{0,1:T(8,128)(2,1)}, bf16[6144,64]{0,1:T(8,128)(2,1)S(1)}, u32[]{:S(2)}) copy-start(bf16[6144,64]{0,1:T(8,128)(2,1)S(1)} %all-reduce.1) | copy-start | bytes 2359300
  207.2 7.8 %copy-start.3 = (f32[768,768]{1,0:T(8,128)S(1)}, f32[768,768]{1,0:T(8,128)}, u32[]{:S(2)}) copy-start(f32[768,768]{1,0:T(8,128)} %param.9) | copy-start | bytes 7077892
Sparse Core Ops, SparseCore 0:
  9.5 49.0 all-gather.3
  75.9 44.1 all-gather.5
